TPU v7x, 32 devices: a whole 2x2x4 slice. The times are simulated.
32 devices in a mesh: cuts: 4 (over x, core), dom: 4 (over z), vec: 2 (over y).
Axes of the slice: x: 2, y: 2, z: 4, core: 2. Of those that a mesh axis runs over, the one named last changes fastest.
Arguments:
- starts_old: bfloat16 [4, 2, 32, 384, 768], P('cuts', None, 'vec', 'dom'), may hold values from -6 to 6
- y_operator: bfloat16 [768, 768], replicated, may hold values from -0.21875 to 0.21875
- coarse_inverse: bfloat16 [384, 384], P('vec'), may hold values from -1 to 2
- base_speed: float32 [384, 768], P('dom'), may hold values from 0.5 to 1.5
- damping: float32 [32], P('vec'), may hold values from 0.5 to 3
- coupling: float32 [32], P('vec'), may hold values from 0.3 to 1.5
Outputs:
- ends_new: float32 [4, 2, 32, 384, 768], P('cuts', None, 'vec', 'dom')
All inputs are finite; a program needn't handle non-finite values.
Results may differ from a plain program's by a relative error of at most 0.0078.
Values may be sent and summed in bfloat16 or wider, within the bound.
No kernel may reach another device: no remote copies, remote signals or barrier semaphores. Data moves between devices by JAX's collectives and lax.ppermute only.
A program may use at most 192 MiB of HBM per device.

v0:
```python
import jax
import jax.numpy as jnp
import numpy as np
from jax import lax
from jax.sharding import PartitionSpec as P

NP = 16
fine_step = 0.25
penalty = 2.0


def from_behind(shard, axis, by):
    size = lax.axis_size(axis)
    pairs = [(i, i + by) for i in range(size) if 0 <= i + by < size]
    return lax.ppermute(shard, axis, pairs)


def cheb_matrix(points_sub):
    indices = np.arange(points_sub)
    points = -np.cos(np.pi * indices / (points_sub - 1))
    edge_weight = np.where((indices == 0) | (indices == points_sub - 1), 2.0, 1.0)
    sign_table = np.where((indices[:, None] + indices[None, :]) % 2 == 0, 1.0, -1.0)
    identity_table = np.eye(points_sub)
    gap_matrix = points[:, None] - points[None, :] + identity_table
    off_diag = (
        edge_weight[:, None]
        / edge_weight[None, :]
        * sign_table
        / gap_matrix
        * (1.0 - identity_table)
    )
    return off_diag - off_diag.sum(axis=1)[:, None] * identity_table


def local(starts_old, y_operator, coarse_inverse, base_speed, damping, coupling):
    start_block = starts_old[0]
    current_state = start_block.astype(jnp.float32)
    part_count, wave_count, column_count, y_count = current_state.shape
    points_sub = NP
    sub_count = column_count // points_sub
    x_scale = 4.0 / (points_sub * points_sub)
    derivative = jnp.asarray(cheb_matrix(points_sub), jnp.float32)
    sign_factor = jnp.array([1.0, -1.0], jnp.float32)[:, None, None, None]
    first_point = (jnp.arange(column_count) % points_sub == 0).astype(jnp.float32)[
        None, None, :, None
    ]
    speed_field = base_speed[None, None]
    full_inverse = lax.all_gather(coarse_inverse, "vec", axis=0, tiled=True)

    def slope_of(values):
        rounded = values.astype(jnp.bfloat16)
        along_y = jnp.dot(
            rounded.reshape(part_count * wave_count * column_count, y_count),
            y_operator,
            preferred_element_type=jnp.float32,
        ).reshape(values.shape)
        blocks = values.reshape(part_count, wave_count, sub_count, points_sub, y_count)
        along_x = jnp.einsum(
            "ij,pwsjy->pwsiy", derivative, blocks, precision=lax.Precision.HIGHEST
        ).reshape(values.shape)
        inflow_row = from_behind(values[:, :, column_count - 1 :, :], "dom", 1)
        previous = jnp.concatenate([inflow_row, values[:, :, : column_count - 1, :]], axis=2)
        jump_term = first_point * (values - previous)
        advect = speed_field * (x_scale * along_x + penalty * jump_term)
        partner = rounded[::-1].astype(jnp.float32)
        return (
            -advect
            + along_y
            + sign_factor * coupling[None, :, None, None] * partner
            - damping[None, :, None, None] * values
        )

    middle = current_state + fine_step * slope_of(current_state)
    fine_end = middle + fine_step * slope_of(middle)
    factor = 1.0 / (1.0 + 2.0 * fine_step * damping)
    is_leader = lax.axis_index("cuts") == 0
    slice_total = lax.axis_size("cuts")
    line_waves = wave_count // lax.axis_size("dom")
    gain = lax.dynamic_slice_in_dim(factor, lax.axis_index("dom") * line_waves, line_waves, 0)[
        None, :, None, None
    ]
    fine_lines = lax.all_to_all(fine_end, "dom", split_axis=1, concat_axis=2, tiled=True)
    start_lines = lax.all_to_all(start_block, "dom", split_axis=1, concat_axis=2, tiled=True)
    line_state = fine_lines
    start_wide = start_lines.astype(jnp.float32)
    for turn_index in range(slice_total - 1):
        arrived = from_behind(line_state.astype(jnp.bfloat16), "cuts", 1)
        gap = (arrived.astype(jnp.float32) - start_wide).astype(jnp.bfloat16)
        mapped = jnp.einsum("ij,pwjy->pwiy", full_inverse, gap, preferred_element_type=jnp.float32)
        line_state = jnp.where(is_leader, fine_lines, fine_lines + gain * mapped)
    block_state = lax.all_to_all(line_state, "dom", split_axis=2, concat_axis=1, tiled=True)
    return block_state[None]


def solution(mesh):
    in_specs = (
        P("cuts", None, "vec", "dom", None),
        P(),
        P("vec", None),
        P("dom", None),
        P("vec"),
        P("vec"),
    )
    out_specs = P("cuts", None, "vec", "dom", None)
    return jax.shard_map(local, mesh=mesh, in_specs=in_specs, out_specs=out_specs, check_vma=False)
```

profile of v0, /device:TPU:1, one launch (start us, length us, event | category | flops | bytes accessed | tf_op | source)
XLA Modules:
  0.0 757.5 jit_solution(18012509088474431244)
XLA Ops:
  0.0 0.0 copy-start
  0.0 0.0 copy-start.9
  0.0 0.0 copy-start.7
  0.0 0.0 copy-start.4
  0.0 0.0 copy-start.8
  0.0 3.6 bitcast_convert_fusion.1
  3.7 0.0 copy-start.5
  3.7 3.7 copy-done.5
  7.4 0.0 copy-start.10
  7.4 0.0 copy-start.11
  7.4 0.1 slice.16
  7.5 4.0 collective-permute-start
  11.6 0.0 copy-done.9
  11.6 0.0 copy-done.8
  11.6 0.1 broadcast_multiply_fusion.2
  11.7 0.0 copy-done.7
  11.7 0.0 copy-done.4
  11.7 6.4 broadcast_multiply_fusion
  18.0 0.0 collective-permute-done
  18.0 0.0 copy-done
  18.0 0.0 copy-done.10
  18.0 0.0 copy-done.11
  18.1 17.1 %fusion.30 = (bf16[2,16,96,768]{3,2,1,0:T(8,128)(2,1)}, f32[2,16,96,768]{3,2,1,0:T(8,128)}) fusion(f32[16]{0:T(128)S(1)} %copy-done.11, bf16[2,16,96,768]{3,2,1,0:T(8,128)(2,1)S(1)} %bitcast.66, f32[2,16]{1,0:T(2,128)S(1)} %broadcast_multiply_fusion.2, bf16[768,768]{1,0:T(8,128)(2,1)S(1)} %copy-done, f32[2,16,95,768]{3,2,1,0:T(8,128)} %bitcast.71, ...), kind=kOutput, calls=%fused_computation.47 | convolution fusion | flops 3663986688 | bytes 39223872 | tf_op jit(solution)/shard_map/dot_general | solution.py:52
  35.1 1.2 slice.18
  36.3 3.4 collective-permute-start.1
  39.7 12.9 %broadcast_multiply_fusion.1 = f32[2,16,6,768,16]{3,4,2,1,0:T(8,128)} fusion(f32[2,16,6,16,768]{4,3,2,1,0:T(8,128)} %bitcast.69, f32[16,16,1,1,1]{1,0,4,3,2:T(8,128)S(1)} %copy-done.7), kind=kOutput, calls=%fused_computation.35 | convolution fusion | flops 455344128 | bytes 18875392 | tf_op jit(solution)/shard_map/ij,pwsjy->pwsiy/dot_general | solution.py:58
  52.6 0.0 collective-permute-done.1
  52.6 19.1 %fusion.21 = f32[2,16,96,768]{3,2,1,0:T(8,128)} fusion(f32[2,16,96,768]{3,2,1,0:T(8,128)} %get-tuple-element.6, f32[2,16,95,768]{3,2,1,0:T(8,128)} %bitcast.70, f32[2,16,1,768]{3,2,1,0:T(1,128)S(1)} %collective-permute-done.1, f32[2,16,6,768,16]{3,4,2,1,0:T(8,128)} %broadcast_multiply_fusion.1, bf16[2,16,96,768]{3,2,1,0:T(8,128)(2,1)} %get-tuple-element.5, ...), kind=kOutput, calls=%fused_computation.26 | convolution fusion | flops 3659268096 | bytes 43942464 | tf_op jit(solution)/shard_map/dot_general | solution.py:52
  71.7 8.4 %copy.50 = f32[2,16,96,768]{3,2,0,1:T(8,128)} copy(f32[2,16,96,768]{3,2,1,0:T(8,128)} %fusion.21) | data formatting | bytes 18874368 | tf_op jit(solution)/shard_map/add | solution.py:74
  80.1 5.8 all-to-all-start
  86.0 4.9 copy.53
  90.8 200.3 %all-to-all-done = f32[2,16,96,768]{3,2,0,1:T(8,128)} async-done(((f32[2,16,96,768]{3,2,0,1:T(8,128)}), f32[2,16,96,768]{3,2,0,1:T(8,128)}, u32[]{:S(2)}, u32[]{:S(2)}) %all-to-all-start) | async-done | bytes 9437216 | tf_op jit(solution)/shard_map/all_to_all | solution.py:82
  291.1 5.0 all-to-all-start.1
  296.1 4.7 copy.52
  300.8 0.0 copy-start.2
  300.8 3.7 copy-done.2
  304.5 0.0 copy-start.6
  304.5 2.7 bitcast_convert_fusion
  307.2 4.4 collective-permute-start.2
  311.6 0.1 dynamic_slice.3
  311.7 0.0 copy-done.6
  311.7 5.9 all_gather.3
  317.6 82.4 %all-to-all-done.1 = bf16[2,16,96,768]{3,2,0,1:T(8,128)(2,1)} async-done(((bf16[2,16,96,768]{3,2,0,1:T(8,128)(2,1)}), bf16[2,16,96,768]{3,2,0,1:T(8,128)(2,1)}, u32[]{:S(2)}, u32[]{:S(2)}) %all-to-all-start.1) | async-done | bytes 4718624 | tf_op jit(solution)/shard_map/all_to_all | solution.py:83
  400.0 2.7 copy.54
  402.7 1.2 convert_bitcast_fusion
  403.9 4.7 copy.55
  408.6 9.6 %copy.64 = f32[2,4,384,768]{2,3,1,0:T(8,128)} copy(f32[2,4,384,768]{3,2,1,0:T(8,128)} %bitcast.61) | data formatting | bytes 18874368 | tf_op jit(solution)/shard_map/all_to_all | solution.py:82
  418.2 0.0 collective-permute-done.2
  418.2 13.9 %fusion = bf16[2,4,384,768]{2,3,1,0:T(8,128)(2,1)} fusion(f32[2,4,384,768]{2,3,1,0:T(8,128)} %copy.64, f32[4]{0:T(128)S(1)} %dynamic_slice.3, pred[]{:T(512)S(6)} %eq.15, f32[2,4,384,768]{3,2,1,0:T(8,128)} %bitcast.62, bf16[2,4,384,768]{3,2,1,0:T(8,128)(2,1)} %collective-permute-done.2, bf16[384,384]{1,0:T(8,128)(2,1)S(1)} %all_gather.3), kind=kOutput, calls=%fused_computation.3 | convolution fusion | flops 1828454400 | bytes 28606480 | tf_op jit(solution)/shard_map/ij,pwjy->pwiy/dot_general | solution.py:89
  432.1 4.4 collective-permute-start.3
  436.5 9.6 %copy.59 = f32[2,4,384,768]{2,3,1,0:T(8,128)} copy(f32[2,4,384,768]{3,2,1,0:T(8,128)} %bitcast.63) | data formatting | bytes 18874368 | tf_op jit(solution)/shard_map/convert_element_type | solution.py:85
  446.1 0.0 copy-start.3
  446.1 41.8 %collective-permute-done.3 = bf16[2,4,384,768]{2,3,1,0:T(8,128)(2,1)} collective-permute-done((bf16[2,4,384,768]{2,3,1,0:T(8,128)(2,1)}, bf16[2,4,384,768]{2,3,1,0:T(8,128)(2,1)}, u32[]{:S(2)}, u32[]{:S(2)}) %collective-permute-start.3) | collective-permute-done | bytes 4718624 | tf_op jit(solution)/shard_map/ppermute | solution.py:15
  487.9 13.5 %fusion.1 = bf16[2,4,384,768]{2,3,1,0:T(8,128)(2,1)} fusion(f32[2,4,384,768]{2,3,1,0:T(8,128)} %copy.64, f32[4]{0:T(128)S(1)} %dynamic_slice.3, pred[]{:T(512)S(6)} %eq.15, f32[2,4,384,768]{2,3,1,0:T(8,128)} %copy.59, bf16[2,4,384,768]{2,3,1,0:T(8,128)(2,1)} %collective-permute-done.3, bf16[384,384]{1,0:T(8,128)(2,1)S(1)} %all_gather.3), kind=kOutput, calls=%fused_computation.4 | convolution fusion | flops 1828454400 | bytes 28606480 | tf_op jit(solution)/shard_map/ij,pwjy->pwiy/dot_general | solution.py:89
  501.4 4.6 collective-permute-start.4
  506.0 51.1 %collective-permute-done.4 = bf16[2,4,384,768]{2,3,1,0:T(8,128)(2,1)S(1)} collective-permute-done((bf16[2,4,384,768]{2,3,1,0:T(8,128)(2,1)}, bf16[2,4,384,768]{2,3,1,0:T(8,128)(2,1)S(1)}, u32[]{:S(2)}, u32[]{:S(2)}) %collective-permute-start.4) | collective-permute-done | bytes 4718624 | tf_op jit(solution)/shard_map/ppermute | solution.py:15
  557.1 0.0 copy-done.3
  557.1 8.0 %add_select_fusion = f32[2,4,384,768]{2,3,1,0:T(8,128)} fusion(f32[2,4,384,768]{2,3,1,0:T(8,128)} %copy.64, f32[4]{0:T(128)S(1)} %dynamic_slice.3, pred[]{:T(512)S(6)} %eq.15, f32[2,4,384,768]{2,3,1,0:T(8,128)S(1)} %copy-done.3, bf16[2,4,384,768]{2,3,1,0:T(8,128)(2,1)S(1)} %collective-permute-done.4, bf16[384,384]{1,0:T(8,128)(2,1)S(1)} %all_gather.3), kind=kOutput, calls=%fused_computation | convolution fusion | flops 1826095104 | bytes 33325072 | tf_op jit(solution)/shard_map/ij,pwjy->pwiy/dot_general | solution.py:89
  565.2 12.5 %copy.65 = f32[2,4,384,768]{3,1,0,2:T(4,128)} copy(f32[2,4,384,768]{2,3,1,0:T(8,128)} %add_select_fusion) | data formatting | bytes 18874368 | tf_op jit(solution)/shard_map/jit(_where)/select_n | solution.py:90
  577.6 164.8 %all_to_all.42 = f32[2,4,384,768]{3,1,0,2:T(4,128)S(1)} all-to-all(f32[2,4,384,768]{3,1,0,2:T(4,128)} %copy.65), channel_id=1, replica_groups=mesh['cuts'=4,'dom'=4,'vec'=2] {'dom'}, dimensions={2} | all-to-all | bytes 18874368 | tf_op jit(solution)/shard_map/all_to_all | solution.py:91
  742.5 6.6 copy.66
  749.0 0.0 copy-start.1
  749.0 8.5 %copy.67 = f32[2,4,4,96,768]{4,3,2,1,0:T(8,128)} copy(f32[2,4,4,96,768]{4,3,1,2,0:T(8,128)} %bitcast.67) | data formatting | bytes 18874368 | tf_op jit(solution)/shard_map/all_to_all | solution.py:91
  757.5 0.0 copy-done.1
  (2 shorter events, 0.0 us)
Async XLA Ops:
  0.0 18.0 %copy-start = (bf16[768,768]{1,0:T(8,128)(2,1)S(1)}, bf16[768,768]{1,0:T(8,128)(2,1)}, u32[]{:S(2)}) copy-start(bf16[768,768]{1,0:T(8,128)(2,1)} %param.9) | copy-start | bytes 3538948
  0.0 11.6 %copy-start.9 = (f32[2]{0:T(128)S(1)}, f32[2]{0:T(128)}, u32[]{:S(2)}) copy-start(f32[2]{0:T(128)} %constant.44.clone) | copy-start | bytes 28
  0.0 11.7 %copy-start.7 = (f32[16,16,1,1,1]{1,0,4,3,2:T(8,128)S(1)}, f32[16,16,1,1,1]{1,0,4,3,2:T(8,128)}, u32[]{:S(2)}) copy-start(f32[16,16,1,1,1]{1,0,4,3,2:T(8,128)} %constant.46) | copy-start | bytes 3076
  0.0 11.6 %copy-start.4 = (bf16[1,2,16,96,768]{4,3,2,1,0:T(8,128)(2,1)S(1)}, bf16[1,2,16,96,768]{4,3,2,1,0:T(8,128)(2,1)}, u32[]{:S(2)}) copy-start(bf16[1,2,16,96,768]{4,3,2,1,0:T(8,128)(2,1)} %param.8) | copy-start | bytes 14155780
  0.0 11.5 %copy-start.8 = (f32[16]{0:T(128)S(1)}, f32[16]{0:T(128)}, u32[]{:S(2)}) copy-start(f32[16]{0:T(128)} %param.13) | copy-start | bytes 196
  3.7 3.7 copy-start.5
  7.4 10.6 %copy-start.10 = (f32[96,768]{1,0:T(8,128)S(1)}, f32[96,768]{1,0:T(8,128)}, u32[]{:S(2)}) copy-start(f32[96,768]{1,0:T(8,128)} %param.11) | copy-start | bytes 884740
  7.4 10.6 %copy-start.11 = (f32[16]{0:T(128)S(1)}, f32[16]{0:T(128)}, u32[]{:S(2)}) copy-start(f32[16]{0:T(128)} %param.12) | copy-start | bytes 196
  7.5 10.5 %collective-permute-start = (f32[2,16,1,768]{3,2,1,0:T(1,128)S(1)}, f32[2,16,1,768]{3,2,1,0:T(1,128)S(1)}, u32[]{:S(2)}, u32[]{:S(2)}) collective-permute-start(f32[2,16,1,768]{3,2,1,0:T(1,128)S(1)} %slice.16), channel_id=1, source_target_pairs={{0,2},{2,4},{4,6},{1,3},{3,5},{5,7},{8,10},{10,12},{12,14},{9,11},... | collective-permute-start | bytes 294920 | tf_op jit(solution)/shard_map/ppermute | solution.py:15
  36.3 16.3 %collective-permute-start.1 = (f32[2,16,1,768]{3,2,1,0:T(1,128)S(1)}, f32[2,16,1,768]{3,2,1,0:T(1,128)S(1)}, u32[]{:S(2)}, u32[]{:S(2)}) collective-permute-start(f32[2,16,1,768]{3,2,1,0:T(1,128)S(1)} %slice.18), channel_id=1, source_target_pairs={{0,2},{2,4},{4,6},{1,3},{3,5},{5,7},{8,10},{10,12},{12,14},{9,11},... | collective-permute-start | bytes 294920 | tf_op jit(solution)/shard_map/ppermute | solution.py:15
  80.1 210.9 %all-to-all-start = ((f32[2,16,96,768]{3,2,0,1:T(8,128)}), f32[2,16,96,768]{3,2,0,1:T(8,128)}, u32[]{:S(2)}, u32[]{:S(2)}) async-start(f32[2,16,96,768]{3,2,0,1:T(8,128)} %copy.50), calls=%async_computation | async-start | bytes 18874368 | tf_op jit(solution)/shard_map/all_to_all | solution.py:82
  291.1 109.0 %all-to-all-start.1 = ((bf16[2,16,96,768]{3,2,0,1:T(8,128)(2,1)}), bf16[2,16,96,768]{3,2,0,1:T(8,128)(2,1)}, u32[]{:S(2)}, u32[]{:S(2)}) async-start(bf16[2,16,96,768]{3,2,0,1:T(8,128)(2,1)} %copy.53), calls=%async_computation.1 | async-start | bytes 9437184 | tf_op jit(solution)/shard_map/all_to_all | solution.py:83
  300.8 3.7 copy-start.2
  304.5 7.2 copy-start.6
  307.2 111.0 %collective-permute-start.2 = (bf16[2,4,384,768]{3,2,1,0:T(8,128)(2,1)}, bf16[2,4,384,768]{3,2,1,0:T(8,128)(2,1)}, u32[]{:S(2)}, u32[]{:S(2)}) collective-permute-start(bf16[2,4,384,768]{3,2,1,0:T(8,128)(2,1)} %bitcast_convert_fusion), channel_id=1, source_target_pairs={{0,8},{8,16},{16,24},{1,9},{9,17},{17,25},{2,10},{10,18},{18,26},{... | collective-permute-start | bytes 14155784 | tf_op jit(solution)/shard_map/ppermute | solution.py:15
  432.1 55.8 %collective-permute-start.3 = (bf16[2,4,384,768]{2,3,1,0:T(8,128)(2,1)}, bf16[2,4,384,768]{2,3,1,0:T(8,128)(2,1)}, u32[]{:S(2)}, u32[]{:S(2)}) collective-permute-start(bf16[2,4,384,768]{2,3,1,0:T(8,128)(2,1)} %fusion), channel_id=1, source_target_pairs={{0,8},{8,16},{16,24},{1,9},{9,17},{17,25},{2,10},{10,18},{18,26},{... | collective-permute-start | bytes 14155784 | tf_op jit(solution)/shard_map/ppermute | solution.py:15
  446.1 111.0 %copy-start.3 = (f32[2,4,384,768]{2,3,1,0:T(8,128)S(1)}, f32[2,4,384,768]{2,3,1,0:T(8,128)}, u32[]{:S(2)}) copy-start(f32[2,4,384,768]{2,3,1,0:T(8,128)} %copy.59) | copy-start | bytes 28311556
  501.4 55.7 %collective-permute-start.4 = (bf16[2,4,384,768]{2,3,1,0:T(8,128)(2,1)}, bf16[2,4,384,768]{2,3,1,0:T(8,128)(2,1)S(1)}, u32[]{:S(2)}, u32[]{:S(2)}) collective-permute-start(bf16[2,4,384,768]{2,3,1,0:T(8,128)(2,1)} %fusion.1), channel_id=1, source_target_pairs={{0,8},{8,16},{16,24},{1,9},{9,17},{17,25},{2,10},{10,18},{18,26},{... | collective-permute-start | bytes 14155784 | tf_op jit(solution)/shard_map/ppermute | solution.py:15
  749.0 8.5 %copy-start.1 = (bf16[768,768]{1,0:T(8,128)(2,1)S(1)}, bf16[768,768]{1,0:T(8,128)(2,1)}, u32[]{:S(2)}) copy-start(bf16[768,768]{1,0:T(8,128)(2,1)} %param.9) | copy-start | bytes 3538948
where the time goes:
time: 759 us; the launch traced here: 758 us
  waiting for transfers between devices  376 us (50%)
  blocking collectives  171 us (23%)
  matrix products  90.9 us (12%)
  local copies, waits for them, and re-layouts  81 us (11%)
  starting transfers between devices  31.6 us (4%)
    all_to_all x1, waiting for transfers between devices, local(): lax.all_to_all(fine_end, 'dom', split_axis=1, concat_axis=2, tiled=True)  200 us
    all_to_all x1, blocking collectives, local(): lax.all_to_all(line_state, 'dom', split_axis=2, concat_axis=1, tiled=True)  165 us
    ppermute x5, waiting for transfers between devices, from_behind(): return lax.ppermute(shard, axis, pairs)  92.9 us
    all_to_all x1, waiting for transfers between devices, local(): lax.all_to_all(start_block, 'dom', split_axis=1, concat_axis=2, tiled=True)  82.4 us
    dot_general x2, matrix products, slope_of(): jnp.dot(rounded.reshape(part_count * wave_count * column_count, y_count),...  36.1 us
    dot_general x3, matrix products, local(): jnp.einsum('ij,pwjy->pwiy', full_inverse, gap, preferred_element_type=jnp...  35.5 us
    ppermute x5, starting transfers between devices, from_behind(): return lax.ppermute(shard, axis, pairs)  20.8 us
    dot_general x2, matrix products, slope_of(): jnp.einsum('ij,pwsjy->pwsiy', derivative, blocks, precision=lax.Precision...  19.3 us
  transfers between devices with their start and end apart: 7, of which 4 were waited for; matrix products, arithmetic and copies ran while one was open for 8% of the time, Pallas kernels for 0%

commit v1 on v0

--- a/solution.py
+++ b/solution.py
@@ -88,7 +88,19 @@
         gap = (arrived.astype(jnp.float32) - start_wide).astype(jnp.bfloat16)
         mapped = jnp.einsum("ij,pwjy->pwiy", full_inverse, gap, preferred_element_type=jnp.float32)
         line_state = jnp.where(is_leader, fine_lines, fine_lines + gain * mapped)
-    block_state = lax.all_to_all(line_state, "dom", split_axis=2, concat_axis=1, tiled=True)
+    ways, here = (lax.axis_size("dom"), lax.axis_index("dom"))
+    width = line_state.shape[2] // ways
+    dims = list(line_state.shape)
+    dims[2] = width
+    height = dims[1]
+    dims[1] = height * ways
+    full = jnp.zeros(dims, line_state.dtype)
+    for mask in range(ways):
+        part = lax.dynamic_slice_in_dim(line_state, (here ^ mask) * width, width, axis=2)
+        if mask:
+            part = lax.ppermute(part, "dom", [(d, d ^ mask) for d in range(ways)])
+        full = lax.dynamic_update_slice_in_dim(full, part, (here ^ mask) * height, axis=1)
+    block_state = full
     return block_state[None]
 
 

time: 759 us -> 728 us (0.959)
  the two profiles are of different devices: /device:TPU:1 before, /device:TPU:10 now
where the time goes in v1:
time: 728 us
  waiting for transfers between devices  537 us (74%)
  matrix products  71.6 us (10%)
  local copies, waits for them, and re-layouts  49.4 us (7%)
  starting transfers between devices  32.2 us (4%)
  other arithmetic  31.4 us (4%)
    all_to_all x1, waiting for transfers between devices, local(): lax.all_to_all(fine_end, 'dom', split_axis=1, concat_axis=2, tiled=True)  197 us
    ppermute x3, waiting for transfers between devices, local(): part = lax.ppermute(part, 'dom', [(d, d ^ mask) for d in range(ways)])  151 us
    ppermute x5, waiting for transfers between devices, from_behind(): return lax.ppermute(shard, axis, pairs)  107 us
    all_to_all x1, waiting for transfers between devices, local(): lax.all_to_all(start_block, 'dom', split_axis=1, concat_axis=2, tiled=True)  81.5 us
    dot_general x2, matrix products, slope_of(): jnp.dot(rounded.reshape(part_count * wave_count * column_count, y_count),...  35.5 us
    convert_element_type x3, other arithmetic, local(): gap = (arrived.astype(jnp.float32) - start_wide).astype(jnp.bfloat16)  25 us
    dot_general x2, matrix products, slope_of(): jnp.einsum('ij,pwsjy->pwsiy', derivative, blocks, precision=lax.Precision...  19.4 us
    dot_general x3, matrix products, local(): jnp.einsum('ij,pwjy->pwiy', full_inverse, gap, preferred_element_type=jnp...  16.7 us
  transfers between devices with their start and end apart: 10, of which 7 were waited for; matrix products, arithmetic and copies ran while one was open for 6% of the time, Pallas kernels for 0%

profile of v1, /device:TPU:10, one launch (start us, length us, event | category | flops | bytes accessed | tf_op | source)
XLA Modules:
  0.0 727.5 jit_solution(13482491418694279199)
XLA Ops:
  0.0 0.0 copy-start
  0.0 0.0 copy-start.3
  0.0 0.0 copy-start.9
  0.0 3.6 bitcast_convert_fusion.1
  3.7 0.0 copy-start.5
  3.7 3.7 copy-done.5
  7.4 0.1 slice.16
  7.5 3.5 collective-permute-start
  11.0 0.1 broadcast_multiply_fusion.2
  11.1 0.0 copy-done.8
  11.1 6.4 broadcast_multiply_fusion
  17.6 0.0 collective-permute-done
  17.6 0.0 copy-done.11
  17.6 0.0 copy-done.12
  17.6 16.7 %fusion.30 = (bf16[2,16,96,768]{3,2,1,0:T(8,128)(2,1)}, f32[2,16,96,768]{3,2,1,0:T(8,128)}) fusion(f32[16]{0:T(128)S(1)} %copy-done.12, bf16[2,16,96,768]{3,2,1,0:T(8,128)(2,1)S(1)} %bitcast.86, f32[2,16]{1,0:T(2,128)S(1)} %broadcast_multiply_fusion.2, bf16[768,768]{1,0:T(8,128)(2,1)S(1)} %copy-done, f32[2,16,95,768]{3,2,1,0:T(8,128)} %bitcast.89, ...), kind=kOutput, calls=%fused_computation.53 | convolution fusion | flops 3663986688 | bytes 39223872 | tf_op jit(solution)/shard_map/dot_general | solution.py:52
  34.3 1.2 slice.18
  35.5 3.7 collective-permute-start.1
  39.2 12.9 %broadcast_multiply_fusion.1 = f32[2,16,6,768,16]{3,4,2,1,0:T(8,128)} fusion(f32[2,16,6,16,768]{4,3,2,1,0:T(8,128)} %bitcast.87, f32[16,16,1,1,1]{1,0,4,3,2:T(8,128)S(1)} %copy-done.8), kind=kOutput, calls=%fused_computation.35 | convolution fusion | flops 455344128 | bytes 18875392 | tf_op jit(solution)/shard_map/ij,pwsjy->pwsiy/dot_general | solution.py:58
  52.1 0.0 collective-permute-done.1
  52.1 18.8 %fusion.21 = f32[2,16,96,768]{3,2,1,0:T(8,128)} fusion(f32[2,16,96,768]{3,2,1,0:T(8,128)} %get-tuple-element.9, f32[2,16,95,768]{3,2,1,0:T(8,128)} %bitcast.88, f32[2,16,1,768]{3,2,1,0:T(1,128)S(1)} %collective-permute-done.1, f32[2,16,6,768,16]{3,4,2,1,0:T(8,128)} %broadcast_multiply_fusion.1, bf16[2,16,96,768]{3,2,1,0:T(8,128)(2,1)} %get-tuple-element.8, ...), kind=kOutput, calls=%fused_computation.26 | convolution fusion | flops 3659268096 | bytes 43942464 | tf_op jit(solution)/shard_map/dot_general | solution.py:52
  70.9 8.4 %copy.11 = f32[2,16,96,768]{3,2,0,1:T(8,128)} copy(f32[2,16,96,768]{3,2,1,0:T(8,128)} %fusion.21) | data formatting | bytes 18874368 | tf_op jit(solution)/shard_map/add | solution.py:74
  79.3 6.2 all-to-all-start
  85.5 4.9 copy.13
  90.4 197.1 %all-to-all-done = f32[2,16,96,768]{3,2,0,1:T(8,128)} async-done(((f32[2,16,96,768]{3,2,0,1:T(8,128)}), f32[2,16,96,768]{3,2,0,1:T(8,128)}, u32[]{:S(2)}, u32[]{:S(2)}) %all-to-all-start) | async-done | bytes 9437216 | tf_op jit(solution)/shard_map/all_to_all | solution.py:82
  287.4 8.3 %all-to-all-start.1 = ((bf16[2,16,96,768]{3,2,0,1:T(8,128)(2,1)}), bf16[2,16,96,768]{3,2,0,1:T(8,128)(2,1)}, u32[]{:S(2)}, u32[]{:S(2)}) async-start(bf16[2,16,96,768]{3,2,0,1:T(8,128)(2,1)} %copy.13), calls=%async_computation.1 | async-start | bytes 9437184 | tf_op jit(solution)/shard_map/all_to_all | solution.py:83
  295.7 4.7 copy.12
  300.4 0.0 copy-start.2
  300.4 3.7 copy-done.2
  304.2 2.6 bitcast_convert_fusion
  306.8 1.9 collective-permute-start.2
  308.7 0.1 dynamic_slice.15
  308.8 0.0 copy-done.7
  308.8 6.0 all_gather.3
  314.8 81.5 %all-to-all-done.1 = bf16[2,16,96,768]{3,2,0,1:T(8,128)(2,1)} async-done(((bf16[2,16,96,768]{3,2,0,1:T(8,128)(2,1)}), bf16[2,16,96,768]{3,2,0,1:T(8,128)(2,1)}, u32[]{:S(2)}, u32[]{:S(2)}) %all-to-all-start.1) | async-done | bytes 4718624 | tf_op jit(solution)/shard_map/all_to_all | solution.py:83
  396.4 7.3 %copy.14 = f32[2,4,4,96,768]{4,3,1,2,0:T(8,128)} copy(bf16[2,4,4,96,768]{4,3,0,2,1:T(8,128)(2,1)} %bitcast.31) | data formatting | bytes 14155776 | tf_op jit(solution)/shard_map/convert_element_type | solution.py:85
  403.7 0.0 collective-permute-done.2
  403.7 8.4 %fusion.22 = bf16[2,4,384,768]{3,2,1,0:T(8,128)(2,1)} fusion(f32[2,4,4,96,768]{4,3,1,2,0:T(8,128)} %copy.14, bf16[2,4,384,768]{3,2,1,0:T(8,128)(2,1)} %collective-permute-done.2), kind=kLoop, calls=%fused_computation.30 | loop fusion | flops 7077888 | bytes 18874368 | tf_op jit(solution)/shard_map/convert_element_type | solution.py:88
  412.1 5.3 fusion
  417.5 1.9 collective-permute-start.3
  419.4 53.6 %collective-permute-done.3 = bf16[2,4,384,768]{3,2,1,0:T(8,128)(2,1)} collective-permute-done((bf16[2,4,384,768]{3,2,1,0:T(8,128)(2,1)S(1)}, bf16[2,4,384,768]{3,2,1,0:T(8,128)(2,1)}, u32[]{:S(2)}, u32[]{:S(2)}) %collective-permute-start.3) | collective-permute-done | bytes 4718624 | tf_op jit(solution)/shard_map/ppermute | solution.py:15
  473.0 8.3 %fusion.23 = bf16[2,4,384,768]{3,2,1,0:T(8,128)(2,1)} fusion(f32[2,4,4,96,768]{4,3,1,2,0:T(8,128)} %copy.14, bf16[2,4,384,768]{3,2,1,0:T(8,128)(2,1)} %collective-permute-done.3), kind=kLoop, calls=%fused_computation.31 | loop fusion | flops 7077888 | bytes 18874368 | tf_op jit(solution)/shard_map/convert_element_type | solution.py:88
  481.4 6.7 fusion.1
  488.1 1.9 collective-permute-start.4
  490.0 0.0 slice-start.3
  490.0 0.0 slice-start.4
  490.0 0.0 slice-start.5
  490.0 53.8 %collective-permute-done.4 = bf16[2,4,384,768]{3,2,1,0:T(8,128)(2,1)} collective-permute-done((bf16[2,4,384,768]{3,2,1,0:T(8,128)(2,1)}, bf16[2,4,384,768]{3,2,1,0:T(8,128)(2,1)}, u32[]{:S(2)}, u32[]{:S(2)}) %collective-permute-start.4) | collective-permute-done | bytes 4718624 | tf_op jit(solution)/shard_map/ppermute | solution.py:15
  543.8 8.3 %fusion.24 = bf16[2,4,384,768]{3,2,1,0:T(8,128)(2,1)} fusion(f32[2,4,4,96,768]{4,3,1,2,0:T(8,128)} %copy.14, bf16[2,4,384,768]{3,2,1,0:T(8,128)(2,1)} %collective-permute-done.4), kind=kLoop, calls=%fused_computation.32 | loop fusion | flops 7077888 | bytes 18874368 | tf_op jit(solution)/shard_map/convert_element_type | solution.py:88
  552.1 4.7 add_select_fusion
  556.8 0.0 copy-start.4
  556.8 3.7 copy-done.4
  560.5 3.0 constant_dynamic-slice_fusion
  563.5 3.4 collective-permute-start.5
  566.9 0.0 collective-permute-start.6
  566.9 1.5 collective-permute-start.7
  568.4 1.1 broadcast_in_dim.20
  569.5 1.9 bitcast_dynamic-update-slice_fusion.3
  571.4 63.8 %collective-permute-done.5 = f32[2,4,96,768]{3,2,1,0:T(8,128)} collective-permute-done((f32[2,4,96,768]{3,2,1,0:T(8,128)}, f32[2,4,96,768]{3,2,1,0:T(8,128)}, u32[]{:S(2)}, u32[]{:S(2)}) %collective-permute-start.5) | collective-permute-done | bytes 2359328 | tf_op jit(solution)/shard_map/ppermute | solution.py:101
  635.1 1.9 bitcast_dynamic-update-slice_fusion.2
  637.0 61.7 %collective-permute-done.6 = f32[2,4,96,768]{3,2,1,0:T(8,128)} collective-permute-done((f32[2,4,96,768]{3,2,1,0:T(8,128)}, f32[2,4,96,768]{3,2,1,0:T(8,128)}, u32[]{:S(2)}, u32[]{:S(2)}) %collective-permute-start.6) | collective-permute-done | bytes 2359328 | tf_op jit(solution)/shard_map/ppermute | solution.py:101
  698.8 1.9 bitcast_dynamic-update-slice_fusion.1
  700.6 0.0 copy-start.6
  700.7 25.2 %collective-permute-done.7 = f32[2,4,96,768]{3,2,1,0:T(8,128)S(1)} collective-permute-done((f32[2,4,96,768]{3,2,1,0:T(8,128)}, f32[2,4,96,768]{3,2,1,0:T(8,128)S(1)}, u32[]{:S(2)}, u32[]{:S(2)}) %collective-permute-start.7) | collective-permute-done | bytes 2359328 | tf_op jit(solution)/shard_map/ppermute | solution.py:101
  725.9 1.7 bitcast_dynamic-update-slice_fusion
  (25 shorter events, 0.1 us)
Async XLA Ops:
  0.0 17.6 %copy-start = (bf16[768,768]{1,0:T(8,128)(2,1)S(1)}, bf16[768,768]{1,0:T(8,128)(2,1)}, u32[]{:S(2)}) copy-start(bf16[768,768]{1,0:T(8,128)(2,1)} %param.9) | copy-start | bytes 3538948
  0.0 11.0 %copy-start.10 = (f32[2]{0:T(128)S(1)}, f32[2]{0:T(128)}, u32[]{:S(2)}) copy-start(f32[2]{0:T(128)} %constant.60.clone) | copy-start | bytes 28
  0.0 11.1 %copy-start.8 = (f32[16,16,1,1,1]{1,0,4,3,2:T(8,128)S(1)}, f32[16,16,1,1,1]{1,0,4,3,2:T(8,128)}, u32[]{:S(2)}) copy-start(f32[16,16,1,1,1]{1,0,4,3,2:T(8,128)} %constant.62) | copy-start | bytes 3076
  0.0 11.1 %copy-start.3 = (bf16[1,2,16,96,768]{4,3,2,1,0:T(8,128)(2,1)S(1)}, bf16[1,2,16,96,768]{4,3,2,1,0:T(8,128)(2,1)}, u32[]{:S(2)}) copy-start(bf16[1,2,16,96,768]{4,3,2,1,0:T(8,128)(2,1)} %param.8) | copy-start | bytes 14155780
  0.0 11.0 %copy-start.9 = (f32[16]{0:T(128)S(1)}, f32[16]{0:T(128)}, u32[]{:S(2)}) copy-start(f32[16]{0:T(128)} %param.13) | copy-start | bytes 196
  3.7 3.7 copy-start.5
  7.4 10.1 %copy-start.11 = (f32[96,768]{1,0:T(8,128)S(1)}, f32[96,768]{1,0:T(8,128)}, u32[]{:S(2)}) copy-start(f32[96,768]{1,0:T(8,128)} %param.11) | copy-start | bytes 884740
  7.4 10.1 %copy-start.12 = (f32[16]{0:T(128)S(1)}, f32[16]{0:T(128)}, u32[]{:S(2)}) copy-start(f32[16]{0:T(128)} %param.12) | copy-start | bytes 196
  7.5 10.0 %collective-permute-start = (f32[2,16,1,768]{3,2,1,0:T(1,128)S(1)}, f32[2,16,1,768]{3,2,1,0:T(1,128)S(1)}, u32[]{:S(2)}, u32[]{:S(2)}) collective-permute-start(f32[2,16,1,768]{3,2,1,0:T(1,128)S(1)} %slice.16), channel_id=1, source_target_pairs={{0,2},{2,4},{4,6},{1,3},{3,5},{5,7},{8,10},{10,12},{12,14},{9,11},... | collective-permute-start | bytes 294920 | tf_op jit(solution)/shard_map/ppermute | solution.py:15
  35.5 16.6 %collective-permute-start.1 = (f32[2,16,1,768]{3,2,1,0:T(1,128)S(1)}, f32[2,16,1,768]{3,2,1,0:T(1,128)S(1)}, u32[]{:S(2)}, u32[]{:S(2)}) collective-permute-start(f32[2,16,1,768]{3,2,1,0:T(1,128)S(1)} %slice.18), channel_id=1, source_target_pairs={{0,2},{2,4},{4,6},{1,3},{3,5},{5,7},{8,10},{10,12},{12,14},{9,11},... | collective-permute-start | bytes 294920 | tf_op jit(solution)/shard_map/ppermute | solution.py:15
  79.3 208.1 %all-to-all-start = ((f32[2,16,96,768]{3,2,0,1:T(8,128)}), f32[2,16,96,768]{3,2,0,1:T(8,128)}, u32[]{:S(2)}, u32[]{:S(2)}) async-start(f32[2,16,96,768]{3,2,0,1:T(8,128)} %copy.11), calls=%async_computation | async-start | bytes 18874368 | tf_op jit(solution)/shard_map/all_to_all | solution.py:82
  287.4 108.9 %all-to-all-start.1 = ((bf16[2,16,96,768]{3,2,0,1:T(8,128)(2,1)}), bf16[2,16,96,768]{3,2,0,1:T(8,128)(2,1)}, u32[]{:S(2)}, u32[]{:S(2)}) async-start(bf16[2,16,96,768]{3,2,0,1:T(8,128)(2,1)} %copy.13), calls=%async_computation.1 | async-start | bytes 9437184 | tf_op jit(solution)/shard_map/all_to_all | solution.py:83
  300.4 3.7 copy-start.2
  304.2 4.7 copy-start.7
  306.8 96.9 %collective-permute-start.2 = (bf16[2,4,384,768]{3,2,1,0:T(8,128)(2,1)}, bf16[2,4,384,768]{3,2,1,0:T(8,128)(2,1)}, u32[]{:S(2)}, u32[]{:S(2)}) collective-permute-start(bf16[2,4,384,768]{3,2,1,0:T(8,128)(2,1)} %bitcast_convert_fusion), channel_id=1, source_target_pairs={{0,8},{8,16},{16,24},{1,9},{9,17},{17,25},{2,10},{10,18},{18,26},{... | collective-permute-start | bytes 14155784 | tf_op jit(solution)/shard_map/ppermute | solution.py:15
  396.4 15.7 %slice-start = ((s8[9437184]{0:T(1024)(128)(4,1)}), s8[4194304]{0:T(1024)(128)(4,1)S(1)}, s32[]{:S(2)}) async-start(s8[9437184]{0:T(1024)(128)(4,1)} %bitcast.80), calls=%async_computation.2 | async-start | bytes 8388608
  396.4 15.7 %slice-start.1 = ((s8[9437184]{0:T(1024)(128)(4,1)}), s8[4194304]{0:T(1024)(128)(4,1)S(1)}, s32[]{:S(2)}) async-start(s8[9437184]{0:T(1024)(128)(4,1)} %bitcast.80), calls=%async_computation.3 | async-start | bytes 8388608
  403.7 8.4 %slice-start.2 = ((s8[9437184]{0:T(1024)(128)(4,1)}), s8[1048576]{0:T(1024)(128)(4,1)S(1)}, s32[]{:S(2)}) async-start(s8[9437184]{0:T(1024)(128)(4,1)} %bitcast.80), calls=%async_computation.4 | async-start | bytes 2097152
  417.5 55.5 %collective-permute-start.3 = (bf16[2,4,384,768]{3,2,1,0:T(8,128)(2,1)S(1)}, bf16[2,4,384,768]{3,2,1,0:T(8,128)(2,1)}, u32[]{:S(2)}, u32[]{:S(2)}) collective-permute-start(bf16[2,4,384,768]{3,2,1,0:T(8,128)(2,1)S(1)} %fusion), channel_id=1, source_target_pairs={{0,8},{8,16},{16,24},{1,9},{9,17},{17,25},{2,10},{10,18},{18,26},{... | collective-permute-start | bytes 14155784 | tf_op jit(solution)/shard_map/ppermute | solution.py:15
  488.1 55.7 %collective-permute-start.4 = (bf16[2,4,384,768]{3,2,1,0:T(8,128)(2,1)}, bf16[2,4,384,768]{3,2,1,0:T(8,128)(2,1)}, u32[]{:S(2)}, u32[]{:S(2)}) collective-permute-start(bf16[2,4,384,768]{3,2,1,0:T(8,128)(2,1)} %fusion.1), channel_id=1, source_target_pairs={{0,8},{8,16},{16,24},{1,9},{9,17},{17,25},{2,10},{10,18},{18,26},{... | collective-permute-start | bytes 14155784 | tf_op jit(solution)/shard_map/ppermute | solution.py:15
  490.0 62.1 %slice-start.3 = ((s8[9437184]{0:T(1024)(128)(4,1)}), s8[1048576]{0:T(1024)(128)(4,1)S(1)}, s32[]{:S(2)}) async-start(s8[9437184]{0:T(1024)(128)(4,1)} %bitcast.82), calls=%async_computation.5 | async-start | bytes 2097152
  490.0 62.1 %slice-start.4 = ((s8[9437184]{0:T(1024)(128)(4,1)}), s8[4194304]{0:T(1024)(128)(4,1)S(1)}, s32[]{:S(2)}) async-start(s8[9437184]{0:T(1024)(128)(4,1)} %bitcast.82), calls=%async_computation.6 | async-start | bytes 8388608
  490.0 62.0 %slice-start.5 = ((s8[9437184]{0:T(1024)(128)(4,1)}), s8[4194304]{0:T(1024)(128)(4,1)S(1)}, s32[]{:S(2)}) async-start(s8[9437184]{0:T(1024)(128)(4,1)} %bitcast.82), calls=%async_computation.7 | async-start | bytes 8388608
  556.8 3.7 copy-start.4
  563.5 71.6 %collective-permute-start.5 = (f32[2,4,96,768]{3,2,1,0:T(8,128)}, f32[2,4,96,768]{3,2,1,0:T(8,128)}, u32[]{:S(2)}, u32[]{:S(2)}) collective-permute-start(f32[2,4,96,768]{3,2,1,0:T(8,128)} %get-tuple-element.7), channel_id=1, source_target_pairs={{0,2},{2,0},{4,6},{6,4},{1,3},{3,1},{5,7},{7,5},{8,10},{10,8},{12,... | collective-permute-start | bytes 7077896 | tf_op jit(solution)/shard_map/ppermute | solution.py:101
  566.9 131.8 %collective-permute-start.6 = (f32[2,4,96,768]{3,2,1,0:T(8,128)}, f32[2,4,96,768]{3,2,1,0:T(8,128)}, u32[]{:S(2)}, u32[]{:S(2)}) collective-permute-start(f32[2,4,96,768]{3,2,1,0:T(8,128)} %get-tuple-element.6), channel_id=1, source_target_pairs={{0,4},{2,6},{4,0},{6,2},{1,5},{3,7},{5,1},{7,3},{8,12},{10,14},{12... | collective-permute-start | bytes 7077896 | tf_op jit(solution)/shard_map/ppermute | solution.py:101
  566.9 158.9 %collective-permute-start.7 = (f32[2,4,96,768]{3,2,1,0:T(8,128)}, f32[2,4,96,768]{3,2,1,0:T(8,128)S(1)}, u32[]{:S(2)}, u32[]{:S(2)}) collective-permute-start(f32[2,4,96,768]{3,2,1,0:T(8,128)} %get-tuple-element.5), channel_id=1, source_target_pairs={{0,6},{2,4},{4,2},{6,0},{1,7},{3,5},{5,3},{7,1},{8,14},{10,12},{12... | collective-permute-start | bytes 7077896 | tf_op jit(solution)/shard_map/ppermute | solution.py:101
  568.4 159.1 %copy-start.1 = (bf16[768,768]{1,0:T(8,128)(2,1)S(1)}, bf16[768,768]{1,0:T(8,128)(2,1)}, u32[]{:S(2)}) copy-start(bf16[768,768]{1,0:T(8,128)(2,1)} %param.9) | copy-start | bytes 3538948
  700.6 25.2 %copy-start.6 = (f32[1,2,16,96,768]{4,3,2,1,0:T(8,128)}, f32[1,2,16,96,768]{4,3,2,1,0:T(8,128)S(1)}, u32[]{:S(2)}) copy-start(f32[1,2,16,96,768]{4,3,2,1,0:T(8,128)S(1)} %bitcast_dynamic-update-slice_fusion.1) | copy-start | bytes 28311556
